TPU v7x, 512 devices: a whole 4x4x16 slice. The times are simulated.
512 devices in a mesh: section: 32 (over y, x, core), inner: 16 (over z).
Axes of the slice: x: 4, y: 4, z: 16, core: 2. Of those that a mesh axis runs over, the one named last changes fastest.
Arguments:
- tokens: bfloat16 [2, 512, 3072], P(None, 'section'), may hold values from -6 to 6
- norm_gain: float32 [3072], replicated, may hold values from 0.5 to 1.5
- router: bfloat16 [3072, 8], replicated, may hold values from -0.21875 to 0.21875
- expert_in: bfloat16 [32, 2, 4096, 3072], P('section', None, 'inner'), may hold values from -0.109375 to 0.109375
- expert_out: bfloat16 [32, 4096, 3072], P('section', 'inner'), may hold values from -0.09375 to 0.09375
- choices: int32 [2, 512, 2], P(None, 'section'), may hold values from 0 to 7, all different within a row; in each aligned block of 16 rows (0 to 15, 16 to 31, ..., all dimensions but the last counted through in order) at most 8 rows name the same one
Outputs:
- layer_outputs: bfloat16 [2, 512, 3072], P(None, 'section', 'inner')
Inputs may be any that keep to these rules, and one draw needn't show every extreme that they name: `choices`: the two experts of a row differ; in each micro-batch the 16 rows of one section name any expert at most 8 times.
All inputs are finite; a program needn't handle non-finite values.
Results may differ from a plain program's by a relative error of at most 0.019.
Values may be sent and summed in bfloat16 or wider, within the bound.
A program may use at most 128 MiB of HBM per device.

v0:
```python
import jax
import jax.numpy as jnp
from jax import lax
from jax.sharding import PartitionSpec as P

epsilon = 1e-05


def prepare(row_block, chosen, norm_scale, router_w, sections, capacity):
    experts = router_w.shape[1]
    model_width = row_block.shape[1]
    values = row_block.astype(jnp.float32)
    inv_rms = lax.rsqrt(jnp.mean(values * values, axis=-1, keepdims=True) + epsilon)
    normed = (values * inv_rms * norm_scale).astype(jnp.bfloat16)
    logits = jnp.dot(normed, router_w, preferred_element_type=jnp.float32)
    expert_ids = jnp.arange(experts, dtype=jnp.int32)
    first_hot = (chosen[:, 0:1] == expert_ids[None, :]).astype(jnp.float32)
    second_hot = (chosen[:, 1:2] == expert_ids[None, :]).astype(jnp.float32)
    lead_logit = jnp.sum(logits * first_hot, axis=1, keepdims=True)
    trail_logit = jnp.sum(logits * second_hot, axis=1, keepdims=True)
    weight_a = 1.0 / (1.0 + jnp.exp(trail_logit - lead_logit))
    weight_b = 1.0 / (1.0 + jnp.exp(lead_logit - trail_logit))
    mixing = weight_a * first_hot + weight_b * second_hot
    hot_count = (chosen[:, 0:1] == expert_ids[None, :]).astype(jnp.int32) + (
        chosen[:, 1:2] == expert_ids[None, :]
    ).astype(jnp.int32)
    slot_rank = jnp.cumsum(hot_count, axis=0) - hot_count
    slot_ids = jnp.arange(capacity, dtype=jnp.int32)
    placed = (
        hot_count[:, :, None] * (slot_rank[:, :, None] == slot_ids[None, None, :]).astype(jnp.int32)
    ).astype(jnp.float32)
    picked = jnp.einsum(
        "rec,rd->ecd", placed.astype(jnp.bfloat16), normed, preferred_element_type=jnp.float32
    ).astype(jnp.bfloat16)
    per_expert = sections // experts
    outgoing = jnp.broadcast_to(picked[:, None], (experts, per_expert, capacity, model_width))
    outgoing = outgoing.reshape(sections, capacity, model_width)
    slot_weights = mixing[:, :, None] * placed
    return (values, outgoing, slot_weights)


def combine(returned_part, slot_weights):
    experts = slot_weights.shape[1]
    capacity = slot_weights.shape[2]
    per_expert = returned_part.shape[0] // experts
    merged = jnp.sum(
        returned_part.astype(jnp.float32).reshape(
            experts, per_expert, capacity, returned_part.shape[2]
        ),
        axis=1,
    )
    return jnp.einsum("rec,ecx->rx", slot_weights, merged, precision=lax.Precision.HIGHEST)


def body(tokens, norm_gain, router, expert_in, expert_out, choices):
    sections = lax.axis_size("section")
    inner_count = lax.axis_size("inner")
    member = lax.axis_index("inner")
    micro_count = tokens.shape[0]
    row_count = tokens.shape[1]
    model_width = tokens.shape[2]
    capacity = row_count // 2
    width_part = model_width // inner_count
    hidden_dev = expert_in.shape[2]
    stacked_in = expert_in[0].reshape(2 * hidden_dev, model_width)
    down_rows = expert_out[0]
    prepared = [
        prepare(tokens[micro_idx], choices[micro_idx], norm_gain, router, sections, capacity)
        for micro_idx in range(micro_count)
    ]
    groups = [[micro_idx] for micro_idx in range(micro_count)]
    results = []
    for batch_group in groups:
        outgoing = jnp.concatenate([prepared[micro_idx][1] for micro_idx in batch_group], axis=1)
        received = lax.all_to_all(outgoing, "section", split_axis=0, concat_axis=0, tiled=True)
        source_count = received.shape[0]
        slot_count = received.shape[1]
        flat_rows = received.reshape(source_count * slot_count, model_width)
        gate_up = lax.dot_general(
            flat_rows, stacked_in, (((1,), (1,)), ((), ())), preferred_element_type=jnp.float32
        )
        active = (jax.nn.silu(gate_up[:, :hidden_dev]) * gate_up[:, hidden_dev:]).astype(
            jnp.bfloat16
        )
        partial_value = jnp.dot(active, down_rows, preferred_element_type=jnp.float32).astype(
            jnp.bfloat16
        )
        partial_value = partial_value.reshape(source_count, slot_count, model_width)
        returned = lax.all_to_all(partial_value, "section", split_axis=0, concat_axis=0, tiled=True)
        combined = jnp.stack(
            [
                combine(returned, prepared[micro_idx][2])
                for index_pos, micro_idx in enumerate(batch_group)
            ]
        )
        moe_part = lax.psum_scatter(
            combined.astype(jnp.bfloat16), "inner", scatter_dimension=2, tiled=True
        ).astype(jnp.float32)
        for index_pos, micro_idx in enumerate(batch_group):
            residual = lax.dynamic_slice_in_dim(
                prepared[micro_idx][0], member * width_part, width_part, 1
            )
            results.append((residual + moe_part[index_pos]).astype(jnp.bfloat16))
    return jnp.stack(results)


def solution(mesh):
    return jax.shard_map(
        body,
        mesh=mesh,
        in_specs=(
            P(None, "section", None),
            P(),
            P(),
            P("section", None, "inner", None),
            P("section", "inner", None),
            P(None, "section", None),
        ),
        out_specs=P(None, "section", "inner"),
        check_vma=False,
    )
```

profile of v0, /device:TPU:6, one launch (start us, length us, event | category | flops | bytes accessed | tf_op | source)
XLA Modules:
  0.0 269.8 jit_solution(304606108101110460)
XLA Ops:
  6.5 0.8 slice_bitcast_fusion.1
  7.4 0.1 copy.17
  7.5 0.1 copy.18
  7.6 1.1 fusion.19
  8.7 1.2 convolution_convert_fusion.2
  9.9 1.3 broadcast_in_dim.5
  11.3 10.3 %all-to-all-start.2 = ((bf16[32,8,3072]{2,1,0:T(8,128)(2,1)}), bf16[32,8,3072]{2,1,0:T(8,128)(2,1)}, u32[]{:S(2)}, u32[]{:S(2)}) async-start(bf16[32,8,3072]{2,1,0:T(8,128)(2,1)} %bitcast.108), calls=%async_computation.2 | async-start | bytes 3145728 | tf_op jit(solution)/shard_map/all_to_all | solution.py:75
  21.6 0.1 copy.13
  21.7 0.1 copy.14
  21.8 1.1 convolution_convert_fusion.3
  22.9 18.7 %all-to-all-done.2 = bf16[32,8,3072]{2,1,0:T(8,128)(2,1)} async-done(((bf16[32,8,3072]{2,1,0:T(8,128)(2,1)}), bf16[32,8,3072]{2,1,0:T(8,128)(2,1)}, u32[]{:S(2)}, u32[]{:S(2)}) %all-to-all-start.2) | async-done | bytes 1572896 | tf_op jit(solution)/shard_map/all_to_all | solution.py:75
  41.6 2.3 broadcast_in_dim.4
  43.9 8.6 %all-to-all-start = ((bf16[32,8,3072]{2,1,0:T(8,128)(2,1)}), bf16[32,8,3072]{2,1,0:T(8,128)(2,1)}, u32[]{:S(2)}, u32[]{:S(2)}) async-start(bf16[32,8,3072]{2,1,0:T(8,128)(2,1)} %bitcast.109), calls=%async_computation | async-start | bytes 3145728 | tf_op jit(solution)/shard_map/all_to_all | solution.py:75
  52.5 0.0 copy-start.1
  52.6 2.5 fusion.6
  55.1 1.8 fusion.1
  56.9 15.7 %all-to-all-done = bf16[32,8,3072]{2,1,0:T(8,128)(2,1)} async-done(((bf16[32,8,3072]{2,1,0:T(8,128)(2,1)}), bf16[32,8,3072]{2,1,0:T(8,128)(2,1)}, u32[]{:S(2)}, u32[]{:S(2)}) %all-to-all-start) | async-done | bytes 1572896 | tf_op jit(solution)/shard_map/all_to_all | solution.py:75
  72.6 8.6 %all-to-all-start.3 = ((bf16[32,8,3072]{2,1,0:T(8,128)(2,1)}), bf16[32,8,3072]{2,1,0:T(8,128)(2,1)}, u32[]{:S(2)}, u32[]{:S(2)}) async-start(bf16[32,8,3072]{2,1,0:T(8,128)(2,1)} %fusion.1), calls=%async_computation.3 | async-start | bytes 3145728 | tf_op jit(solution)/shard_map/all_to_all | solution.py:89
  81.2 0.0 copy-start.2
  81.2 2.5 fusion.10
  83.7 1.8 fusion
  85.5 15.7 %all-to-all-done.3 = bf16[32,8,3072]{2,1,0:T(8,128)(2,1)} async-done(((bf16[32,8,3072]{2,1,0:T(8,128)(2,1)}), bf16[32,8,3072]{2,1,0:T(8,128)(2,1)}, u32[]{:S(2)}, u32[]{:S(2)}) %all-to-all-start.3) | async-done | bytes 1572896 | tf_op jit(solution)/shard_map/all_to_all | solution.py:89
  101.2 8.6 %all-to-all-start.1 = ((bf16[32,8,3072]{2,1,0:T(8,128)(2,1)}), bf16[32,8,3072]{2,1,0:T(8,128)(2,1)}, u32[]{:S(2)}, u32[]{:S(2)}) async-start(bf16[32,8,3072]{2,1,0:T(8,128)(2,1)} %fusion), calls=%async_computation.1 | async-start | bytes 3145728 | tf_op jit(solution)/shard_map/all_to_all | solution.py:89
  109.8 0.0 reduce-scatter.9.cloned.1.call-start
  109.9 0.2 select_reduce_fusion.1
  110.1 0.2 select_reduce_fusion.3
  110.4 1.7 convert_reduce_fusion
  112.1 0.9 fusion.4
  113.0 2.9 %copy.23 = bf16[1,16,3072]{1,0,2:T(2,128)(2,1)} copy(bf16[1,16,3072]{2,1,0:T(8,128)(2,1)S(1)} %fusion.4) | data formatting | bytes 196608
  115.9 2.4 copy.37
  118.3 0.0 reduce-scatter.9.cloned.1.call-update
  118.4 0.0 reduce-scatter.7.cloned.1.call-start
  118.4 11.4 %all-to-all-done.1 = bf16[32,8,3072]{2,1,0:T(8,128)(2,1)} async-done(((bf16[32,8,3072]{2,1,0:T(8,128)(2,1)}), bf16[32,8,3072]{2,1,0:T(8,128)(2,1)}, u32[]{:S(2)}, u32[]{:S(2)}) %all-to-all-start.1) | async-done | bytes 1572896 | tf_op jit(solution)/shard_map/all_to_all | solution.py:89
  129.8 1.7 convert_reduce_fusion.1
  131.6 0.9 fusion.5
  132.5 2.9 %copy.21 = bf16[1,16,3072]{1,0,2:T(2,128)(2,1)} copy(bf16[1,16,3072]{2,1,0:T(8,128)(2,1)S(1)} %fusion.5) | data formatting | bytes 196608
  135.4 2.4 copy.38
  137.8 0.0 reduce-scatter.7.cloned.1.call-update
  137.8 0.7 slice_convert_fusion.1
  138.5 51.4 %reduce-scatter.9.cloned.1.call-done = bf16[192,16]{1,0:T(8,128)(2,1)} async-done(((bf16[3072,16]{1,0:T(8,128)(2,1)}), bf16[192,16]{1,0:T(8,128)(2,1)}) %reduce-scatter.9.cloned.1.call-update) | async-done | bytes 6160
  189.9 0.9 reshape_bitcast_fusion
  190.8 0.1 copy.24
  190.9 69.7 %reduce-scatter.7.cloned.1.call-done = bf16[192,16]{1,0:T(8,128)(2,1)} async-done(((bf16[3072,16]{1,0:T(8,128)(2,1)}), bf16[192,16]{1,0:T(8,128)(2,1)}) %reduce-scatter.7.cloned.1.call-update) | async-done | bytes 6160
  260.6 0.9 reshape_bitcast_fusion.1
  261.4 0.1 copy.22
  261.5 0.8 add_convert_fusion
  262.3 0.1 add_convert_fusion.1
  262.4 0.6 pad_maximum_fusion
  (24 shorter events, 0.2 us)
Async XLA Ops:
  6.5 46.0 %copy-start = (bf16[1,2,256,3072]{3,2,1,0:T(8,128)(2,1)S(1)}, bf16[1,2,256,3072]{3,2,1,0:T(8,128)(2,1)}, u32[]{:S(2)}) copy-start(bf16[1,2,256,3072]{3,2,1,0:T(8,128)(2,1)} %param.9) | copy-start | bytes 9437188
  11.3 10.5 %copy-start.3 = (bf16[2,16,3072]{2,1,0:T(8,128)(2,1)S(1)}, bf16[2,16,3072]{2,1,0:T(8,128)(2,1)}, u32[]{:S(2)}) copy-start(bf16[2,16,3072]{2,1,0:T(8,128)(2,1)} %param.6) | copy-start | bytes 589828
  11.3 10.5 %copy-start.4 = (f32[3072]{0:T(1024)S(1)}, f32[3072]{0:T(1024)}, u32[]{:S(2)}) copy-start(f32[3072]{0:T(1024)} %param.7) | copy-start | bytes 36868
  11.3 30.3 %all-to-all-start.2 = ((bf16[32,8,3072]{2,1,0:T(8,128)(2,1)}), bf16[32,8,3072]{2,1,0:T(8,128)(2,1)}, u32[]{:S(2)}, u32[]{:S(2)}) async-start(bf16[32,8,3072]{2,1,0:T(8,128)(2,1)} %bitcast.108), calls=%async_computation.2 | async-start | bytes 3145728 | tf_op jit(solution)/shard_map/all_to_all | solution.py:75
  43.9 28.6 %all-to-all-start = ((bf16[32,8,3072]{2,1,0:T(8,128)(2,1)}), bf16[32,8,3072]{2,1,0:T(8,128)(2,1)}, u32[]{:S(2)}, u32[]{:S(2)}) async-start(bf16[32,8,3072]{2,1,0:T(8,128)(2,1)} %bitcast.109), calls=%async_computation | async-start | bytes 3145728 | tf_op jit(solution)/shard_map/all_to_all | solution.py:75
  52.5 2.6 copy-start.1
  72.6 28.6 %all-to-all-start.3 = ((bf16[32,8,3072]{2,1,0:T(8,128)(2,1)}), bf16[32,8,3072]{2,1,0:T(8,128)(2,1)}, u32[]{:S(2)}, u32[]{:S(2)}) async-start(bf16[32,8,3072]{2,1,0:T(8,128)(2,1)} %fusion.1), calls=%async_computation.3 | async-start | bytes 3145728 | tf_op jit(solution)/shard_map/all_to_all | solution.py:89
  81.2 2.6 copy-start.2
  85.5 24.4 %copy-start.5 = (bf16[3072,8]{0,1:T(8,128)(2,1)S(1)}, bf16[3072,8]{0,1:T(8,128)(2,1)}, u32[]{:S(2)}) copy-start(bf16[3072,8]{0,1:T(8,128)(2,1)} %param.8) | copy-start | bytes 147460
  101.2 28.6 %all-to-all-start.1 = ((bf16[32,8,3072]{2,1,0:T(8,128)(2,1)}), bf16[32,8,3072]{2,1,0:T(8,128)(2,1)}, u32[]{:S(2)}, u32[]{:S(2)}) async-start(bf16[32,8,3072]{2,1,0:T(8,128)(2,1)} %fusion), calls=%async_computation.1 | async-start | bytes 3145728 | tf_op jit(solution)/shard_map/all_to_all | solution.py:89
  109.8 80.1 %reduce-scatter.9.cloned.1.call-start = ((), (), s32[]{:S(2)}) async-start(), calls=%async_computation.7 | async-start | bytes 835584
  118.4 142.2 %reduce-scatter.7.cloned.1.call-start = ((), (), s32[]{:S(2)}) async-start(), calls=%async_computation.6 | async-start | bytes 835584
Sparse Core Ops, SparseCore 0:
  118.5 71.4 reduce-scatter.8
  193.0 67.5 reduce-scatter.6
where the time goes:
time: 271 us; the launch traced here: 270 us
  waiting for transfers between devices  183 us (68%)
  starting transfers between devices  36.2 us (13%)
  local copies, waits for them, and re-layouts  17.3 us (6%)
  between operations  13.6 us (5%)
  matrix products  13.2 us (5%)
  other arithmetic  6.94 us (3%)
    unnamed x4, waiting for transfers between devices  121 us
    all_to_all x2, waiting for transfers between devices, body(): lax.all_to_all(outgoing, 'section', split_axis=0, concat_axis=0, tiled=True)  34.4 us
    all_to_all x2, waiting for transfers between devices, body(): lax.all_to_all(partial_value, 'section', split_axis=0, concat_axis=0, til...  27.1 us
    all_to_all x2, starting transfers between devices, body(): lax.all_to_all(outgoing, 'section', split_axis=0, concat_axis=0, tiled=True)  18.9 us
    all_to_all x2, starting transfers between devices, body(): lax.all_to_all(partial_value, 'section', split_axis=0, concat_axis=0, til...  17.2 us
    unnamed x20, local copies, waits for them, and re-layouts  12.5 us
  transfers between devices with their start and end apart: 6, of which 6 were waited for; matrix products, arithmetic and copies ran while one was open for 10% of the time, Pallas kernels for 0%

commit v1 on v0

v1 whole, which is shorter than its diff:
```python
import functools
import math

import jax
import jax.numpy as jnp
from jax import lax
from jax.experimental import pallas as pl
from jax.experimental.pallas import tpu as pltpu
from jax.sharding import PartitionSpec as P

epsilon = 1e-05
MESH = pl.DeviceIdType.MESH
BF16 = jnp.bfloat16
F32 = jnp.float32


def nt_dot(a, b):
    return lax.dot_general(a, b, (((1,), (1,)), ((), ())), preferred_element_type=F32)


def moe_kernel(
    sections,
    inners,
    experts,
    micro,
    tokens,
    gain,
    router,
    choices,
    w_in,
    w_out,
    out,
    normed,
    outgoing,
    slots,
    w_in_v,
    w_out_v,
    gate_up,
    active,
    mix_hi,
    mix_lo,
    pair_send,
    pair_recv,
    own,
    deep_send,
    deep_recv,
    back_send,
    back_recv,
    part_send,
    part_recv,
    w_sem,
    out_sem,
    in_sem,
    deep_out_sem,
    deep_in_sem,
    share_out_sem,
    share_in_sem,
    pair_out_sem,
    pair_in_sem,
    fold_out_sem,
    fold_in_sem,
    back_out_sem,
    back_in_sem,
    part_out_sem,
    part_in_sem,
):
    chips = sections // 2
    side = math.isqrt(chips)
    per_expert = chips // experts
    rows_all, width = tokens.shape
    rows = rows_all // micro
    cap = rows // 2
    tile = micro * cap
    q_width = width // 4
    hidden = w_out.shape[0]
    half_rows = chips * tile
    group_rows = side * tile
    slice_width = width // inners
    per_quarter = inners // 4

    section = lax.axis_index("section")
    z = lax.axis_index("inner")
    chip, core = section // 2, lax.rem(section, 2)
    chip_y, chip_x = chip // side, lax.rem(chip, side)
    parity = lax.rem(z, 2)
    z_up = lax.rem(z + 1, inners)
    z_down = lax.rem(z + inners - 1, inners)
    partner = chip * 2 + 1 - core
    deep_to = (z_up, z_down)
    fold_to = (z_down, z_up)
    mine = pl.multiple_of(core * half_rows, half_rows)
    theirs = pl.multiple_of((1 - core) * half_rows, half_rows)
    keep = (2 * parity, 2 * parity + 1)
    pass_on = (2 * (1 - parity), 2 * (1 - parity) + 1)

    def local(src, dst, sem):
        return pltpu.make_async_copy(src, dst, sem)

    def remote(src, dst, send, recv, to_section, to_inner):
        return pltpu.make_async_remote_copy(
            src_ref=src, dst_ref=dst, send_sem=send, recv_sem=recv, device_id=(to_section, to_inner), device_id_type=MESH
        )

    def took(view, sem):
        local(view, view, sem).wait()

    for q in range(4):
        local(w_in.at[:, pl.ds(q * q_width, q_width)], w_in_v.at[q], w_sem.at[q]).start()
    for q in range(4):
        local(w_out.at[:, pl.ds(q * q_width, q_width)], w_out_v.at[q], w_sem.at[4 + q]).start()

    offsets = [(dy, dx) for dy in range(side) for dx in range(side) if (dy, dx) != (0, 0)]
    offsets.sort(key=lambda o: (min(o[0], side - o[0]) + min(o[1], side - o[1]), o))

    def chip_at(dy, dx):
        return lax.rem(chip_y + dy, side) * side + lax.rem(chip_x + dx, side)

    barrier = pltpu.get_barrier_semaphore()
    for dy, dx in offsets:
        pl.semaphore_signal(barrier, inc=1, device_id=(chip_at(dy, dx) * 2 + core, z), device_id_type=MESH)
    pl.semaphore_signal(barrier, inc=1, device_id=(partner, z), device_id_type=MESH)
    for k in range(1, inners):
        pl.semaphore_signal(barrier, inc=1, device_id=(section, lax.rem(z + k, inners)), device_id_type=MESH)

    values = tokens[...].astype(F32)
    inv_rms = lax.rsqrt(jnp.mean(values * values, axis=-1, keepdims=True) + epsilon)
    normed_value = (values * inv_rms * gain[...]).astype(BF16)
    for q in range(4):
        normed[q] = normed_value[:, q * q_width : (q + 1) * q_width]
    logits = jnp.dot(normed_value, router[...], preferred_element_type=F32)
    first, second = choices[:, 0:1], choices[:, 1:2]

    def hot(index, name):
        return jnp.where(index == name, 1.0, 0.0).astype(F32)

    ids = lax.broadcasted_iota(jnp.int32, (rows_all, experts), 1)
    lead = jnp.sum(logits * hot(first, ids), axis=1, keepdims=True)
    trail = jnp.sum(logits * hot(second, ids), axis=1, keepdims=True)
    weight_a = 1.0 / (1.0 + jnp.exp(trail - lead))
    weight_b = 1.0 / (1.0 + jnp.exp(lead - trail))
    row_of = lax.broadcasted_iota(jnp.int32, (rows_all, rows_all), 0)
    col_of = lax.broadcasted_iota(jnp.int32, (rows_all, rows_all), 1)
    before = jnp.where((row_of // rows == col_of // rows) & (col_of < row_of), 1.0, 0.0).astype(BF16)

    def placing(columns, copies):
        col = lax.broadcasted_iota(jnp.int32, (rows_all, columns), 1)
        row = lax.broadcasted_iota(jnp.int32, (rows_all, columns), 0)
        name = col // (tile * copies)
        first_hot, second_hot = hot(first, name), hot(second, name)
        both = first_hot + second_hot
        rank = jnp.dot(before, both.astype(BF16), preferred_element_type=F32)
        seat = (lax.rem(col, tile) // cap == row // rows) & (rank == lax.rem(col, cap).astype(F32))
        return jnp.where(seat, both, 0.0), jnp.where(seat, weight_a * first_hot + weight_b * second_hot, 0.0)

    placed, _ = placing(experts * tile, 1)
    _, mixing = placing(chips * tile, per_expert)
    mixing_high = mixing.astype(BF16)
    mix_hi[...] = mixing_high
    mix_lo[...] = (mixing - mixing_high.astype(F32)).astype(BF16)
    placed_t = jnp.transpose(placed).astype(BF16)
    for i in range(2):
        picked = jnp.dot(placed_t, normed[keep[i]], preferred_element_type=F32).astype(BF16)
        outgoing[i] = picked.reshape(experts, tile, q_width)
    home = pl.multiple_of(mine + chip * tile, tile)
    for i in range(2):
        slots[keep[i], pl.ds(home, tile), :] = outgoing[i, chip // per_expert]

    pl.semaphore_wait(barrier, len(offsets) + 1 + inners - 1)

    for dy, dx in offsets:
        to = chip_at(dy, dx)
        for i in range(2):
            remote(
                outgoing.at[i, to // per_expert],
                slots.at[keep[i], pl.ds(home, tile), :],
                out_sem.at[0],
                in_sem.at[i, chip_y],
                to * 2 + core,
                z,
            ).start()

    def group_at(j):
        return lax.rem(chip_y + j, side)

    def group_of(j):
        return pl.ds(pl.multiple_of(mine + group_at(j) * group_rows, group_rows), group_rows)

    for j in range(side):
        for i in range(2):
            arrived = group_rows if j else group_rows - tile
            took(slots.at[keep[i], pl.ds(0, arrived), :], in_sem.at[i, group_at(j)])
            view = slots.at[keep[i], group_of(j), :]
            remote(view, view, deep_out_sem.at[0], deep_in_sem.at[i, group_at(j)], section, deep_to[i]).start()
            remote(view, view, share_out_sem.at[0], share_in_sem.at[0, i], partner, z).start()

    def project(q):
        for half in range(2):
            block = pl.ds(half * half_rows, half_rows)
            gate_up[block, :] += nt_dot(slots[q, block, :], w_in_v[q])

    gate_up[...] = jnp.zeros_like(gate_up)
    for q in range(4):
        took(w_in_v.at[q], w_sem.at[q])
    for i in range(2):
        took(slots.at[keep[i], pl.ds(0, half_rows), :], share_in_sem.at[0, i])
        project(keep[i])
    for j in range(side):
        for i in range(2):
            took(slots.at[pass_on[i], pl.ds(0, group_rows), :], deep_in_sem.at[i, group_at(j)])
            view = slots.at[pass_on[i], group_of(j), :]
            remote(view, view, share_out_sem.at[0], share_in_sem.at[1, i], partner, z).start()
    for i in range(2):
        took(slots.at[pass_on[i], pl.ds(0, half_rows), :], share_in_sem.at[1, i])
        project(pass_on[i])

    gate = gate_up[:, :hidden]
    active[...] = (gate / (1.0 + jnp.exp(-gate)) * gate_up[:, hidden:]).astype(BF16)

    for q in range(4):
        took(w_out_v.at[q], w_sem.at[4 + q])
    order = pass_on + keep
    for n, q in enumerate(order):
        pair_send[n] = jnp.dot(active[pl.ds(theirs, half_rows), :], w_out_v[q], preferred_element_type=F32).astype(BF16)
        remote(pair_send.at[n], pair_recv.at[n], pair_out_sem.at[0], pair_in_sem.at[n], partner, z).start()
    for n, q in enumerate(order):
        own[n] = jnp.dot(active[pl.ds(mine, half_rows), :], w_out_v[q], preferred_element_type=F32).astype(BF16)

    for i in range(2):
        took(pair_recv.at[i], pair_in_sem.at[i])
        deep_send[i] = (own[i].astype(F32) + pair_recv[i].astype(F32)).astype(BF16)
        remote(deep_send.at[i], deep_recv.at[i], fold_out_sem.at[0], fold_in_sem.at[i], section, fold_to[i]).start()
    for i in range(2):
        took(pair_recv.at[2 + i], pair_in_sem.at[2 + i])
        took(deep_recv.at[i], fold_in_sem.at[i])
        total = own[2 + i].astype(F32) + pair_recv[2 + i].astype(F32) + deep_recv[i].astype(F32)
        back_send[i] = total.astype(BF16)
        here = pl.ds(pl.multiple_of(chip * tile, tile), tile)
        back_recv[i, here, :] = back_send[i, here, :]
        for dy, dx in offsets:
            to = chip_at(dy, dx)
            there = pl.ds(pl.multiple_of(to * tile, tile), tile)
            remote(
                back_send.at[i, there, :], back_recv.at[i, here, :], back_out_sem.at[0], back_in_sem.at[i], to * 2 + core, z
            ).start()

    for i in range(2):
        took(back_recv.at[i, pl.ds(0, half_rows - tile), :], back_in_sem.at[i])
        total = jnp.dot(mix_hi[...], back_recv[i], preferred_element_type=F32) + jnp.dot(
            mix_lo[...], back_recv[i], preferred_element_type=F32
        )
        for j in range(per_quarter):
            shifted = total if j == 0 else pltpu.roll(total, q_width - j * slice_width, 1)
            n = i * per_quarter + j
            part_send[n] = shifted[:, :slice_width].astype(BF16)
            to = parity * (inners // 2) + n

            @pl.when(to == z)
            def _():
                local(part_send.at[n], part_recv.at[z // 2], part_in_sem.at[0]).start()

            @pl.when(to != z)
            def _():
                remote(part_send.at[n], part_recv.at[z // 2], part_out_sem.at[0], part_in_sem.at[0], section, to).start()

    took(part_recv, part_in_sem.at[0])
    total = part_recv[0].astype(F32)
    for k in range(1, inners // 2):
        total += part_recv[k].astype(F32)
    out[...] = total

    took(back_send.at[:, pl.ds(0, half_rows - tile), :], out_sem.at[0])
    took(back_send, deep_out_sem.at[0])
    took(pair_send, share_out_sem.at[0])
    took(pair_send, pair_out_sem.at[0])
    took(deep_send, fold_out_sem.at[0])
    took(back_send.at[:, pl.ds(0, half_rows - tile), :], back_out_sem.at[0])
    inside = z // (inners // 2) == parity

    @pl.when(inside)
    def _():
        took(part_send.at[pl.ds(0, inners // 2 - 1)], part_out_sem.at[0])

    @pl.when(jnp.logical_not(inside))
    def _():
        took(part_send, part_out_sem.at[0])


def body(tokens, norm_gain, router, expert_in, expert_out, choices):
    sections = lax.axis_size("section")
    inners = lax.axis_size("inner")
    member = lax.axis_index("inner")
    micro, rows, width = tokens.shape
    experts = router.shape[1]
    hidden = expert_in.shape[2]
    chips = sections // 2
    side = math.isqrt(chips)
    slice_width = width // inners
    q_width = width // 4
    rows_all = micro * rows
    tile = micro * (rows // 2)
    half_rows = chips * tile
    flat = tokens.reshape(rows_all, width)
    vmem = pl.BlockSpec(memory_space=pltpu.VMEM)
    anywhere = pl.BlockSpec(memory_space=pl.ANY)
    dma = pltpu.SemaphoreType.DMA
    moe = pl.pallas_call(
        functools.partial(moe_kernel, sections, inners, experts, micro),
        out_shape=jax.ShapeDtypeStruct((rows_all, slice_width), F32),
        in_specs=[vmem, vmem, vmem, vmem, anywhere, anywhere],
        out_specs=vmem,
        scratch_shapes=[
            pltpu.VMEM((4, rows_all, q_width), BF16),
            pltpu.VMEM((2, experts, tile, q_width), BF16),
            pltpu.VMEM((4, 2 * half_rows, q_width), BF16),
            pltpu.VMEM((4, 2 * hidden, q_width), BF16),
            pltpu.VMEM((4, hidden, q_width), BF16),
            pltpu.VMEM((2 * half_rows, 2 * hidden), F32),
            pltpu.VMEM((2 * half_rows, hidden), BF16),
            pltpu.VMEM((rows_all, half_rows), BF16),
            pltpu.VMEM((rows_all, half_rows), BF16),
            pltpu.VMEM((4, half_rows, q_width), BF16),
            pltpu.VMEM((4, half_rows, q_width), BF16),
            pltpu.VMEM((4, half_rows, q_width), BF16),
            pltpu.VMEM((2, half_rows, q_width), BF16),
            pltpu.VMEM((2, half_rows, q_width), BF16),
            pltpu.VMEM((2, half_rows, q_width), BF16),
            pltpu.VMEM((2, half_rows, q_width), BF16),
            pltpu.VMEM((inners // 2, rows_all, slice_width), BF16),
            pltpu.VMEM((inners // 2, rows_all, slice_width), BF16),
            dma((8,)),
            dma((1,)),
            dma((2, side)),
            dma((1,)),
            dma((2, side)),
            dma((1,)),
            dma((2, 2)),
            dma((1,)),
            dma((4,)),
            dma((1,)),
            dma((2,)),
            dma((1,)),
            dma((2,)),
            dma((1,)),
            dma((1,)),
        ],
        compiler_params=pltpu.CompilerParams(
            collective_id=0, has_side_effects=True, vmem_limit_bytes=48 * 1024 * 1024
        ),
    )(
        flat,
        norm_gain.reshape(1, width),
        router,
        choices.reshape(rows_all, 2),
        expert_in.reshape(2 * hidden, width),
        expert_out.reshape(hidden, width),
    )
    residual = lax.dynamic_slice_in_dim(flat, member * slice_width, slice_width, 1).astype(F32)
    return (residual + moe).astype(BF16).reshape(micro, rows, slice_width)


def solution(mesh):
    return jax.shard_map(
        body,
        mesh=mesh,
        in_specs=(
            P(None, "section", None),
            P(),
            P(),
            P("section", None, "inner", None),
            P("section", "inner", None),
            P(None, "section", None),
        ),
        out_specs=P(None, "section", "inner"),
        check_vma=False,
    )
```

time: 271 us -> 73 us (0.27)
  waiting for transfers between devices: 183 us -> 0 us
  Pallas kernels: 0 us -> 64.2 us
  starting transfers between devices: 36.2 us -> 0 us
  between operations: 13.6 us -> 0.03 us
  matrix products: 13.2 us -> 0 us
  local copies, waits for them, and re-layouts: 17.3 us -> 6.86 us
  other arithmetic: 6.94 us -> 1.43 us
    unnamed x4 -> x0, waiting for transfers between devices: 121 us -> none
    pallas_call x0 -> x1, Pallas kernels: none -> 64.2 us  [body(): pl.pallas_call(functools.partial(moe_kernel, sections, inners, experts, m...]
    all_to_all x4 -> x0, waiting for transfers between devices: 61.5 us -> none  [the longest x2 34.4 us: body(): lax.all_to_all(outgoing, 'section', split_axis=0, concat_axis=0, tiled=True)]
    all_to_all x4 -> x0, starting transfers between devices: 36.1 us -> none  [the longest x2 18.9 us: body(): lax.all_to_all(outgoing, 'section', split_axis=0, concat_axis=0, tiled=True)]
    dot_general x10 -> x0, matrix products: 13.2 us -> none  [the longest x2 5.08 us: body(): lax.dot_general(flat_rows, stacked_in, (((1,), (1,)), ((), ())), preferre...]
    unnamed x20 -> x9, local copies, waits for them, and re-layouts: 12.5 us -> 6.1 us
    reduce_sum x3 -> x0, other arithmetic: 4.55 us -> none  [the longest x2 3.46 us: combine(): jnp.sum(returned_part.astype(jnp.float32).reshape(experts, per_expert, ca...]
    broadcast_in_dim x2 -> x0, local copies, waits for them, and re-layouts: 3.64 us -> none  [prepare(): jnp.broadcast_to(picked[:, None], (experts, per_expert, capacity, model_w...]
  transfers between devices with their start and end apart: 6 -> 0, of which waited for: 6 -> 0; matrix products, arithmetic and copies ran while one was open for 10% -> 0% of each run, Pallas kernels for 0% -> 0%
where the time goes in v1:
time: 73 us; the launch traced here: 72.5 us
  Pallas kernels  64.2 us (88%)
  local copies, waits for them, and re-layouts  6.86 us (9%)
  other arithmetic  1.43 us (2%)
    pallas_call x1, Pallas kernels, body(): pl.pallas_call(functools.partial(moe_kernel, sections, inners, experts, m...  64.2 us
    unnamed x9, local copies, waits for them, and re-layouts  6.1 us

profile of v1, /device:TPU:6, one launch (start us, length us, event | category | flops | bytes accessed | tf_op | source)
XLA Modules:
  0.0 72.5 jit_solution(5056738941177074186)
XLA Ops:
  0.0 1.2 %copy.8.router = bf16[3072,8]{1,0:T(8,128)(2,1)S(1)} copy(bf16[3072,8]{0,1:T(8,128)(2,1)} %param.8) | data formatting | bytes 98304 | tf_op args[2]
  1.2 0.8 %copy.10 = s32[2,16,2]{2,1,0:T(8,128)S(1)} copy(s32[2,16,2]{1,2,0:T(2,128)} %param.11) | data formatting | bytes 512 | tf_op jit(solution)/shard_map/reshape | solution.py:353
  1.9 0.0 copy-start
  1.9 1.9 %copy-done = bf16[1,2,256,3072]{3,2,1,0:T(8,128)(2,1)S(1)} copy-done((bf16[1,2,256,3072]{3,2,1,0:T(8,128)(2,1)S(1)}, bf16[1,2,256,3072]{3,2,1,0:T(8,128)(2,1)}, u32[]{:S(2)}) %copy-start) | copy-done | bytes 3145752
  3.8 0.0 copy-start.1
  3.8 1.4 %copy-done.1 = bf16[1,256,3072]{2,1,0:T(8,128)(2,1)S(1)} copy-done((bf16[1,256,3072]{2,1,0:T(8,128)(2,1)S(1)}, bf16[1,256,3072]{2,1,0:T(8,128)(2,1)}, u32[]{:S(2)}) %copy-start.1) | copy-done | bytes 1572888
  5.2 0.0 copy-start.2
  5.2 0.9 %copy-done.2 = bf16[2,16,3072]{2,1,0:T(8,128)(2,1)S(1)} copy-done((bf16[2,16,3072]{2,1,0:T(8,128)(2,1)S(1)}, bf16[2,16,3072]{2,1,0:T(8,128)(2,1)}, u32[]{:S(2)}) %copy-start.2) | copy-done | bytes 196632
  6.2 0.0 copy-start.3
  6.2 0.7 copy-done.3
  6.9 64.2 %shard_map.64 = f32[32,192]{1,0:T(8,128)S(1)} custom-call(bf16[32,3072]{1,0:T(8,128)(2,1)S(1)} %bitcast.9, f32[1,3072]{1,0:T(1,128)S(1)} %bitcast.11, bf16[3072,8]{1,0:T(8,128)(2,1)S(1)} %copy.8.router, s32[32,2]{1,0:T(8,128)S(1)} %bitcast.10, bf16[512,3072]{1,0:T(8,128)(2,1)S(1)} %bitcast.6, bf16[256,3072]{1,0:T(8,128)(2,1)S(1)} %bitcast.7), custom_call_target="tpu_custom_call" | custom-call | tf_op jit(solution)/shard_map/pallas_call | solution.py:306
  71.1 1.4 %add_convert_fusion = bf16[32,192]{1,0:T(8,128)(2,1)} fusion(f32[32,192]{1,0:T(8,128)S(1)} %shard_map.64, bf16[32,3072]{1,0:T(8,128)(2,1)} %bitcast.8, s32[]{:T(128)S(6)} %select_n.3), kind=kLoop, calls=%fused_computation | loop fusion | flops 18432 | bytes 49156 | tf_op jit(solution)/shard_map/convert_element_type | solution.py:358
Async XLA Ops:
  1.9 1.9 %copy-start = (bf16[1,2,256,3072]{3,2,1,0:T(8,128)(2,1)S(1)}, bf16[1,2,256,3072]{3,2,1,0:T(8,128)(2,1)}, u32[]{:S(2)}) copy-start(bf16[1,2,256,3072]{3,2,1,0:T(8,128)(2,1)} %param.9) | copy-start | bytes 9437188
  3.8 1.4 %copy-start.1 = (bf16[1,256,3072]{2,1,0:T(8,128)(2,1)S(1)}, bf16[1,256,3072]{2,1,0:T(8,128)(2,1)}, u32[]{:S(2)}) copy-start(bf16[1,256,3072]{2,1,0:T(8,128)(2,1)} %param.10) | copy-start | bytes 4718596
  5.2 0.9 %copy-start.2 = (bf16[2,16,3072]{2,1,0:T(8,128)(2,1)S(1)}, bf16[2,16,3072]{2,1,0:T(8,128)(2,1)}, u32[]{:S(2)}) copy-start(bf16[2,16,3072]{2,1,0:T(8,128)(2,1)} %param.6) | copy-start | bytes 589828
  6.2 0.7 copy-start.3

commit v2 on v1

v2 whole, which is shorter than its diff:
```python
import functools
import math

import jax
import jax.numpy as jnp
from jax import lax
from jax.experimental import pallas as pl
from jax.experimental.pallas import tpu as pltpu
from jax.sharding import PartitionSpec as P

epsilon = 1e-05
MESH = pl.DeviceIdType.MESH
BF16 = jnp.bfloat16
F32 = jnp.float32


def nt_dot(a, b):
    return lax.dot_general(a, b, (((1,), (1,)), ((), ())), preferred_element_type=F32)


def moe_kernel(
    sections,
    inners,
    experts,
    micro,
    tokens_hbm,
    gain_hbm,
    router_hbm,
    choices_hbm,
    w_in,
    w_out,
    out,
    tokens,
    gain,
    router,
    choices,
    normed,
    outgoing,
    slots,
    w_in_v,
    w_out_v,
    active,
    mix,
    partial,
    pair_recv,
    deep_send,
    deep_recv,
    back_send,
    back_recv,
    part_send,
    part_recv,
    residual,
    small_sem,
    w_sem,
    out_sem,
    in_sem,
    deep_out_sem,
    deep_in_sem,
    share_out_sem,
    share_in_sem,
    pair_out_sem,
    pair_in_sem,
    fold_out_sem,
    fold_in_sem,
    back_out_sem,
    back_in_sem,
    part_out_sem,
    part_in_sem,
):
    chips = sections // 2
    side = math.isqrt(chips)
    per_expert = chips // experts
    rows_all, width = tokens.shape
    rows = rows_all // micro
    cap = rows // 2
    tile = micro * cap
    q_width = width // 4
    hidden = w_out.shape[0]
    half_rows = chips * tile
    group_rows = side * tile
    slice_width = width // inners
    per_quarter = inners // 4

    section = lax.axis_index("section")
    z = lax.axis_index("inner")
    chip, core = section // 2, lax.rem(section, 2)
    chip_y, chip_x = chip // side, lax.rem(chip, side)
    parity = lax.rem(z, 2)
    z_up = lax.rem(z + 1, inners)
    z_down = lax.rem(z + inners - 1, inners)
    partner = chip * 2 + 1 - core
    deep_to = (z_up, z_down)
    fold_to = (z_down, z_up)
    keep = 2 * parity
    pass_on = 2 * (1 - parity)

    def local(src, dst, sem):
        return pltpu.make_async_copy(src, dst, sem)

    def remote(src, dst, send, recv, to_section, to_inner):
        return pltpu.make_async_remote_copy(
            src_ref=src, dst_ref=dst, send_sem=send, recv_sem=recv, device_id=(to_section, to_inner), device_id_type=MESH
        )

    def took(view, sem):
        local(view, view, sem).wait()

    small = ((tokens_hbm, tokens), (gain_hbm, gain), (router_hbm, router), (choices_hbm, choices))
    for n, (src, dst) in enumerate(small):
        local(src, dst, small_sem.at[n]).start()
    for q in range(4):
        local(w_in.at[:, pl.ds(q * q_width, q_width)], w_in_v.at[q], w_sem.at[q]).start()
    for q in range(4):
        local(w_out.at[:, pl.ds(q * q_width, q_width)], w_out_v.at[q], w_sem.at[4 + q]).start()

    steps = sorted(range(side), key=lambda j: (j % 2, j))
    offsets = [(-j % side, dx) for j in steps for dx in range(side) if (j, dx) != (0, 0)]

    def place_of(y):
        return lax.rem(y, 2) * (side // 2) + y // 2

    my_place = place_of(chip_y)

    def chip_at(dy, dx):
        return lax.rem(chip_y + dy, side) * side + lax.rem(chip_x + dx, side)

    barrier = pltpu.get_barrier_semaphore()
    for dy, dx in offsets:
        pl.semaphore_signal(barrier, inc=1, device_id=(chip_at(dy, dx) * 2 + core, z), device_id_type=MESH)
    pl.semaphore_signal(barrier, inc=1, device_id=(partner, z), device_id_type=MESH)
    for k in range(1, inners):
        pl.semaphore_signal(barrier, inc=1, device_id=(section, lax.rem(z + k, inners)), device_id_type=MESH)

    for n, (src, dst) in enumerate(small):
        local(src, dst, small_sem.at[n]).wait()
    values = tokens[...].astype(F32)
    inv_rms = lax.rsqrt(jnp.mean(values * values, axis=-1, keepdims=True) + epsilon)
    normed_value = (values * inv_rms * gain[...]).astype(BF16)
    for q in range(4):
        normed[q] = normed_value[:, q * q_width : (q + 1) * q_width]
    row_of = lax.broadcasted_iota(jnp.int32, (rows, rows_all), 0)
    col_of = lax.broadcasted_iota(jnp.int32, (rows, rows_all), 1)
    chosen = jnp.zeros((2, rows_all), F32)
    for m in range(micro):
        spread = jnp.where(col_of == row_of + m * rows, 1.0, 0.0).astype(BF16)
        chosen += jnp.dot(choices[m].astype(F32).astype(BF16), spread, preferred_element_type=F32)
    first, second = chosen[0:1].astype(jnp.int32), chosen[1:2].astype(jnp.int32)
    row_of = lax.broadcasted_iota(jnp.int32, (rows_all, rows_all), 0)
    col_of = lax.broadcasted_iota(jnp.int32, (rows_all, rows_all), 1)
    before = jnp.where((row_of // rows == col_of // rows) & (row_of < col_of), 1.0, 0.0).astype(BF16)

    def hot(index, name):
        return jnp.where(index == name, 1.0, 0.0).astype(F32)

    def seats(count, copies):
        seat_of = lax.broadcasted_iota(jnp.int32, (count, rows_all), 0)
        row_of = lax.broadcasted_iota(jnp.int32, (count, rows_all), 1)
        name = seat_of // (tile * copies)
        first_hot, second_hot = hot(first, name), hot(second, name)
        rank = jnp.dot((first_hot + second_hot).astype(BF16), before, preferred_element_type=F32)
        seat = (lax.rem(seat_of, tile) // cap == row_of // rows) & (rank == lax.rem(seat_of, cap).astype(F32))
        return first_hot, second_hot, seat

    first_hot, second_hot, seat = seats(experts * tile, 1)
    placed = jnp.where(seat, first_hot + second_hot, 0.0).astype(BF16)
    for i in range(2):
        picked = jnp.dot(placed, normed[keep + i], preferred_element_type=F32).astype(BF16)
        outgoing[:, i] = picked.reshape(experts, tile, q_width)
    both = pl.ds(keep, 2)
    home = pl.ds(pl.multiple_of((my_place * 2 + core) * group_rows + chip_x * tile, tile), tile)
    slots[both, home, :] = outgoing[chip // per_expert]

    pl.semaphore_wait(barrier, len(offsets) + 1 + inners - 1)

    for dy, dx in offsets:
        to = chip_at(dy, dx)
        remote(
            outgoing.at[to // per_expert], slots.at[both, home, :], out_sem.at[0], in_sem.at[my_place], to * 2 + core, z
        ).start()

    logits = nt_dot(router[...], normed_value)
    ids = lax.broadcasted_iota(jnp.int32, (experts, rows_all), 0)
    lead = jnp.sum(logits * hot(first, ids), axis=0, keepdims=True)
    trail = jnp.sum(logits * hot(second, ids), axis=0, keepdims=True)
    weight_a = 1.0 / (1.0 + jnp.exp(trail - lead))
    weight_b = 1.0 / (1.0 + jnp.exp(lead - trail))
    first_hot, second_hot, seat = seats(chips * tile, per_expert)
    mixing = jnp.transpose(jnp.where(seat, weight_a * first_hot + weight_b * second_hot, 0.0))
    mixing_high = mixing.astype(BF16)
    mix[:rows_all, :] = mixing_high
    mix[rows_all:, :] = (mixing - mixing_high.astype(F32)).astype(BF16)
    lane = 128
    base = pl.multiple_of(z * slice_width // lane * lane, lane)
    window = tokens[:, pl.ds(base, 2 * lane)].astype(F32)
    moved = pltpu.roll(window, 2 * lane - slice_width % lane, 1)
    residual[...] = jnp.where(z * slice_width == base, window, moved)[:, :slice_width]

    def rows_of(g, c):
        return pl.ds(pl.multiple_of((g * 2 + c) * group_rows, group_rows), group_rows)

    def group_of(g):
        return pl.ds(pl.multiple_of(g * group_rows, group_rows), group_rows)

    def swap_planes(j):
        g = place_of(lax.rem(chip_y + j, side))
        arrived = group_rows if j else group_rows - tile
        took(slots.at[both, pl.ds(0, arrived), :], in_sem.at[g])
        here = rows_of(g, core)
        for i in range(2):
            view = slots.at[keep + i, here, :]
            remote(view, view, deep_out_sem.at[0], deep_in_sem.at[i, g], section, deep_to[i]).start()
        view = slots.at[both, here, :]
        remote(view, view, share_out_sem.at[0], share_in_sem.at[0, g], partner, z).start()

    def share(j):
        g = place_of(lax.rem(chip_y + j, side))
        here = rows_of(g, core)
        for i in range(2):
            took(slots.at[pass_on + i, here, :], deep_in_sem.at[i, g])
        view = slots.at[pl.ds(pass_on, 2), here, :]
        remote(view, view, share_out_sem.at[0], share_in_sem.at[1, g], partner, z).start()

    def compute(j):
        pair = pl.multiple_of(lax.rem(chip_y + j, 2) * half_rows, half_rows)
        block = pl.ds(pair, half_rows)
        first_group = lax.rem(chip_y + j, 2) * (side // 2)
        for n in range(2):
            for m in range(side // 2):
                view = slots.at[pl.ds(0, 2), rows_of(first_group + m, 1 - core), :]
                took(view, share_in_sem.at[n, first_group + m])
        gate_up = nt_dot(slots[0, block, :], w_in_v[0])
        for q in range(1, 4):
            gate_up += nt_dot(slots[q, block, :], w_in_v[q])
        gate = gate_up[:, :hidden]
        active[block, :] = (gate / (1.0 + jnp.exp(-gate)) * gate_up[:, hidden:]).astype(BF16)
        for half, first_q in enumerate((pass_on, keep)):
            for i in range(2):
                partial[2 * half + i, block, :] = jnp.dot(
                    active[block, :], w_out_v[first_q + i], preferred_element_type=F32
                ).astype(BF16)
            for m in range(side // 2):
                g = first_group + m
                remote(
                    partial.at[pl.ds(2 * half, 2), rows_of(g, 1 - core), :],
                    pair_recv.at[pl.ds(2 * half, 2), group_of(g), :],
                    pair_out_sem.at[0],
                    pair_in_sem.at[half, g],
                    partner,
                    z,
                ).start()

    def fold(j):
        g = place_of(lax.rem(chip_y + j, side))
        here = group_of(g)
        took(pair_recv.at[pl.ds(0, 2), here, :], pair_in_sem.at[0, g])
        for i in range(2):
            total = partial[i, rows_of(g, core), :].astype(F32) + pair_recv[i, here, :].astype(F32)
            deep_send[i, here, :] = total.astype(BF16)
            remote(
                deep_send.at[i, here, :], deep_recv.at[i, here, :], fold_out_sem.at[0], fold_in_sem.at[i, g], section, fold_to[i]
            ).start()

    def give_back(j, i):
        g = place_of(lax.rem(chip_y + j, side))
        here = group_of(g)
        if i == 0:
            took(pair_recv.at[pl.ds(2, 2), here, :], pair_in_sem.at[1, g])
        took(deep_recv.at[i, here, :], fold_in_sem.at[i, g])
        total = partial[2 + i, rows_of(g, core), :].astype(F32) + pair_recv[2 + i, here, :].astype(F32)
        back_send[i, here, :] = (total + deep_recv[i, here, :].astype(F32)).astype(BF16)
        landing = pl.ds(pl.multiple_of(chip * tile, tile), tile)
        for dx in range(side):
            x = lax.rem(chip_x + dx, side)
            there = pl.ds(pl.multiple_of(g * group_rows + x * tile, tile), tile)
            if (j, dx) == (0, 0):
                back_recv[i, landing, :] = back_send[i, there, :]
            else:
                remote(
                    back_send.at[i, there, :],
                    back_recv.at[i, landing, :],
                    back_out_sem.at[0],
                    back_in_sem.at[i],
                    chip_at(j, dx) * 2 + core,
                    z,
                ).start()

    for q in range(4):
        took(w_in_v.at[q], w_sem.at[q])
        took(w_out_v.at[q], w_sem.at[4 + q])
    order_of_work = (
        (swap_planes, 0),
        (swap_planes, 1),
        (share, 0),
        (swap_planes, 2),
        (swap_planes, 3),
        (share, 1),
        (compute, 0),
        (share, 2),
        (fold, 0),
        (fold, 1),
        (share, 3),
        (compute, 2),
        (give_back, 0, 0),
        (give_back, 0, 1),
        (give_back, 1, 0),
        (give_back, 1, 1),
        (fold, 2),
        (fold, 3),
        (give_back, 2, 0),
        (give_back, 3, 0),
        (give_back, 2, 1),
        (give_back, 3, 1),
    )
    for work, *which in order_of_work:
        work(steps[which[0]], *which[1:])

    for i in range(2):
        took(back_recv.at[i, pl.ds(0, half_rows - tile), :], back_in_sem.at[i])
        parts = jnp.dot(mix[...], back_recv[i], preferred_element_type=F32)
        total = parts[:rows_all] + parts[rows_all:]
        for j in range(per_quarter):
            shifted = total if j == 0 else pltpu.roll(total, q_width - j * slice_width, 1)
            part_send[i * per_quarter + j] = shifted[:, :slice_width].astype(BF16)
        for away in sorted(range(inners), key=lambda d: -min(d, inners - d)):
            to = lax.rem(z + away, inners)

            @pl.when(to // per_quarter == keep + i)
            def _():
                n = lax.rem(to, inners // 2)
                if away == 0:
                    local(part_send.at[n], part_recv.at[z // 2], part_in_sem.at[0]).start()
                else:
                    remote(part_send.at[n], part_recv.at[z // 2], part_out_sem.at[0], part_in_sem.at[0], section, to).start()

    took(part_recv, part_in_sem.at[0])
    total = residual[...]
    for k in range(inners // 2):
        total += part_recv[k].astype(F32)
    out[...] = total.astype(BF16)

    took(back_send.at[:, pl.ds(0, half_rows - tile), :], out_sem.at[0])
    took(back_send, deep_out_sem.at[0])
    took(pair_recv, share_out_sem.at[0])
    took(pair_recv, pair_out_sem.at[0])
    took(deep_send, fold_out_sem.at[0])
    took(back_send.at[:, pl.ds(0, half_rows - tile), :], back_out_sem.at[0])
    inside = z // (inners // 2) == parity

    @pl.when(inside)
    def _():
        took(part_send.at[pl.ds(0, inners // 2 - 1)], part_out_sem.at[0])

    @pl.when(jnp.logical_not(inside))
    def _():
        took(part_send, part_out_sem.at[0])


def body(tokens, norm_gain, router, expert_in, expert_out, choices):
    sections = lax.axis_size("section")
    inners = lax.axis_size("inner")
    micro, rows, width = tokens.shape
    experts = router.shape[1]
    hidden = expert_in.shape[2]
    chips = sections // 2
    side = math.isqrt(chips)
    slice_width = width // inners
    q_width = width // 4
    rows_all = micro * rows
    tile = micro * (rows // 2)
    half_rows = chips * tile
    vmem = pl.BlockSpec(memory_space=pltpu.VMEM)
    anywhere = pl.BlockSpec(memory_space=pl.ANY)
    dma = pltpu.SemaphoreType.DMA
    moe = pl.pallas_call(
        functools.partial(moe_kernel, sections, inners, experts, micro),
        out_shape=jax.ShapeDtypeStruct((rows_all, slice_width), BF16),
        in_specs=[anywhere] * 6,
        out_specs=vmem,
        scratch_shapes=[
            pltpu.VMEM((rows_all, width), BF16),
            pltpu.VMEM((1, width), F32),
            pltpu.VMEM((experts, width), BF16),
            pltpu.VMEM((micro, 2, rows), jnp.int32),
            pltpu.VMEM((4, rows_all, q_width), BF16),
            pltpu.VMEM((experts, 2, tile, q_width), BF16),
            pltpu.VMEM((4, 2 * half_rows, q_width), BF16),
            pltpu.VMEM((4, 2 * hidden, q_width), BF16),
            pltpu.VMEM((4, hidden, q_width), BF16),
            pltpu.VMEM((2 * half_rows, hidden), BF16),
            pltpu.VMEM((2 * rows_all, half_rows), BF16),
            pltpu.VMEM((4, 2 * half_rows, q_width), BF16),
            pltpu.VMEM((4, half_rows, q_width), BF16),
            pltpu.VMEM((2, half_rows, q_width), BF16),
            pltpu.VMEM((2, half_rows, q_width), BF16),
            pltpu.VMEM((2, half_rows, q_width), BF16),
            pltpu.VMEM((2, half_rows, q_width), BF16),
            pltpu.VMEM((inners // 2, rows_all, slice_width), BF16),
            pltpu.VMEM((inners // 2, rows_all, slice_width), BF16),
            pltpu.VMEM((rows_all, slice_width), F32),
            dma((4,)),
            dma((8,)),
            dma((1,)),
            dma((side,)),
            dma((1,)),
            dma((2, side)),
            dma((1,)),
            dma((2, side)),
            dma((1,)),
            dma((2, side)),
            dma((1,)),
            dma((2, side)),
            dma((1,)),
            dma((2,)),
            dma((1,)),
            dma((1,)),
        ],
        compiler_params=pltpu.CompilerParams(
            collective_id=0, has_side_effects=True, vmem_limit_bytes=62 * 1024 * 1024
        ),
    )(
        tokens.reshape(rows_all, width),
        norm_gain.reshape(1, width),
        router.T,
        jnp.swapaxes(choices, 1, 2),
        expert_in.reshape(2 * hidden, width),
        expert_out.reshape(hidden, width),
    )
    return moe.reshape(micro, rows, slice_width)


def solution(mesh):
    return jax.shard_map(
        body,
        mesh=mesh,
        in_specs=(
            P(None, "section", None),
            P(),
            P(),
            P("section", None, "inner", None),
            P("section", "inner", None),
            P(None, "section", None),
        ),
        out_specs=P(None, "section", "inner"),
        check_vma=False,
    )
```

time: 73 us -> 59.7 us (0.82)
  the two profiles are of different devices: /device:TPU:6 before, /device:TPU:8 now
where the time goes in v2:
time: 59.7 us; the launch traced here: 59.5 us
  Pallas kernels  58.2 us (97%)
  local copies, waits for them, and re-layouts  1.32 us (2%)
    pallas_call x1, Pallas kernels, body(): pl.pallas_call(functools.partial(moe_kernel, sections, inners, experts, m...  58.2 us
    unnamed x1, local copies, waits for them, and re-layouts  1.32 us

profile of v2, /device:TPU:8, one launch (start us, length us, event | category | flops | bytes accessed | tf_op | source)
XLA Modules:
  0.0 59.5 jit_solution(8363446807832961753)
XLA Ops:
  0.0 58.2 %shard_map.64 = bf16[32,192]{1,0:T(8,128)(2,1)} custom-call(bf16[32,3072]{1,0:T(8,128)(2,1)} %bitcast.9, f32[1,3072]{1,0:T(1,128)} %bitcast.12, bf16[8,3072]{1,0:T(8,128)(2,1)} %bitcast.11, s32[2,2,16]{2,1,0:T(2,128)} %bitcast.13, bf16[512,3072]{1,0:T(8,128)(2,1)} %bitcast.7, bf16[256,3072]{1,0:T(8,128)(2,1)} %bitcast.8), custom_call_target="tpu_custom_call" | custom-call | tf_op jit(solution)/shard_map/pallas_call | solution.py:374
  58.2 1.3 %copy.8 = bf16[2,16,192]{2,1,0:T(8,128)(2,1)} copy(bf16[2,16,192]{2,1,0:T(8,128)(2,1)} %bitcast.10) | data formatting | bytes 24576

commit v3 on v2

--- a/solution.py
+++ b/solution.py
@@ -77,7 +77,9 @@
     q_width = width // 4
     hidden = w_out.shape[0]
     half_rows = chips * tile
-    group_rows = side * tile
+    halves = side // 2
+    batch = side // 2 * halves
+    group_rows = 2 * tile
     slice_width = width // inners
     per_quarter = inners // 4
 
@@ -114,19 +116,25 @@
         local(w_out.at[:, pl.ds(q * q_width, q_width)], w_out_v.at[q], w_sem.at[4 + q]).start()
 
     steps = sorted(range(side), key=lambda j: (j % 2, j))
-    offsets = [(-j % side, dx) for j in steps for dx in range(side) if (j, dx) != (0, 0)]
-
-    def place_of(y):
-        return lax.rem(y, 2) * (side // 2) + y // 2
-
-    my_place = place_of(chip_y)
-
-    def chip_at(dy, dx):
-        return lax.rem(chip_y + dy, side) * side + lax.rem(chip_x + dx, side)
+
+    chip_pair = chip_x // 2
+    sibling = 1 - 2 * lax.rem(chip_x, 2)
+
+    def group_at(j, h):
+        y = lax.rem(chip_y + j, side)
+        return (lax.rem(y, 2) * (side // 2) + y // 2) * halves + lax.rem(chip_pair + h, halves)
+
+    def chips_at(j, h):
+        y, x = lax.rem(chip_y + j, side), lax.rem(chip_x + 2 * h, side)
+        return [(y * side + x + n * sibling, x + n * sibling) for n in range(2) if (j, h, n) != (0, 0, 0)]
+
+    my_group = group_at(0, 0)
 
     barrier = pltpu.get_barrier_semaphore()
-    for dy, dx in offsets:
-        pl.semaphore_signal(barrier, inc=1, device_id=(chip_at(dy, dx) * 2 + core, z), device_id_type=MESH)
+    for j in steps:
+        for h in range(halves):
+            for to, _ in chips_at(j, h):
+                pl.semaphore_signal(barrier, inc=1, device_id=(to * 2 + core, z), device_id_type=MESH)
     pl.semaphore_signal(barrier, inc=1, device_id=(partner, z), device_id_type=MESH)
     for k in range(1, inners):
         pl.semaphore_signal(barrier, inc=1, device_id=(section, lax.rem(z + k, inners)), device_id_type=MESH)
@@ -167,16 +175,17 @@
         picked = jnp.dot(placed, normed[keep + i], preferred_element_type=F32).astype(BF16)
         outgoing[:, i] = picked.reshape(experts, tile, q_width)
     both = pl.ds(keep, 2)
-    home = pl.ds(pl.multiple_of((my_place * 2 + core) * group_rows + chip_x * tile, tile), tile)
+    home = pl.ds(pl.multiple_of((my_group * 2 + core) * group_rows + lax.rem(chip_x, 2) * tile, tile), tile)
     slots[both, home, :] = outgoing[chip // per_expert]
 
-    pl.semaphore_wait(barrier, len(offsets) + 1 + inners - 1)
-
-    for dy, dx in offsets:
-        to = chip_at(dy, dx)
-        remote(
-            outgoing.at[to // per_expert], slots.at[both, home, :], out_sem.at[0], in_sem.at[my_place], to * 2 + core, z
-        ).start()
+    pl.semaphore_wait(barrier, chips - 1 + 1 + inners - 1)
+
+    for j in steps:
+        for h in range(halves):
+            for to, _ in chips_at(-j % side, h):
+                remote(
+                    outgoing.at[to // per_expert], slots.at[both, home, :], out_sem.at[0], in_sem.at[my_group], to * 2 + core, z
+                ).start()
 
     logits = nt_dot(router[...], normed_value)
     ids = lax.broadcasted_iota(jnp.int32, (experts, rows_all), 0)
@@ -201,9 +210,9 @@
     def group_of(g):
         return pl.ds(pl.multiple_of(g * group_rows, group_rows), group_rows)
 
-    def swap_planes(j):
-        g = place_of(lax.rem(chip_y + j, side))
-        arrived = group_rows if j else group_rows - tile
+    def swap_planes(j, h):
+        g = group_at(j, h)
+        arrived = len(chips_at(j, h)) * tile
         took(slots.at[both, pl.ds(0, arrived), :], in_sem.at[g])
         here = rows_of(g, core)
         for i in range(2):
@@ -212,8 +221,8 @@
         view = slots.at[both, here, :]
         remote(view, view, share_out_sem.at[0], share_in_sem.at[0, g], partner, z).start()
 
-    def share(j):
-        g = place_of(lax.rem(chip_y + j, side))
+    def share(j, h):
+        g = group_at(j, h)
         here = rows_of(g, core)
         for i in range(2):
             took(slots.at[pass_on + i, here, :], deep_in_sem.at[i, g])
@@ -223,9 +232,9 @@
     def compute(j):
         pair = pl.multiple_of(lax.rem(chip_y + j, 2) * half_rows, half_rows)
         block = pl.ds(pair, half_rows)
-        first_group = lax.rem(chip_y + j, 2) * (side // 2)
+        first_group = lax.rem(chip_y + j, 2) * batch
         for n in range(2):
-            for m in range(side // 2):
+            for m in range(batch):
                 view = slots.at[pl.ds(0, 2), rows_of(first_group + m, 1 - core), :]
                 took(view, share_in_sem.at[n, first_group + m])
         gate_up = nt_dot(slots[0, block, :], w_in_v[0])
@@ -238,7 +247,7 @@
                 partial[2 * half + i, block, :] = jnp.dot(
                     active[block, :], w_out_v[first_q + i], preferred_element_type=F32
                 ).astype(BF16)
-            for m in range(side // 2):
+            for m in range(batch):
                 g = first_group + m
                 remote(
                     partial.at[pl.ds(2 * half, 2), rows_of(g, 1 - core), :],
@@ -249,8 +258,8 @@
                     z,
                 ).start()
 
-    def fold(j):
-        g = place_of(lax.rem(chip_y + j, side))
+    def fold(j, h):
+        g = group_at(j, h)
         here = group_of(g)
         took(pair_recv.at[pl.ds(0, 2), here, :], pair_in_sem.at[0, g])
         for i in range(2):
@@ -260,8 +269,8 @@
                 deep_send.at[i, here, :], deep_recv.at[i, here, :], fold_out_sem.at[0], fold_in_sem.at[i, g], section, fold_to[i]
             ).start()
 
-    def give_back(j, i):
-        g = place_of(lax.rem(chip_y + j, side))
+    def give_back(j, h, i):
+        g = group_at(j, h)
         here = group_of(g)
         if i == 0:
             took(pair_recv.at[pl.ds(2, 2), here, :], pair_in_sem.at[1, g])
@@ -269,50 +278,69 @@
         total = partial[2 + i, rows_of(g, core), :].astype(F32) + pair_recv[2 + i, here, :].astype(F32)
         back_send[i, here, :] = (total + deep_recv[i, here, :].astype(F32)).astype(BF16)
         landing = pl.ds(pl.multiple_of(chip * tile, tile), tile)
-        for dx in range(side):
-            x = lax.rem(chip_x + dx, side)
-            there = pl.ds(pl.multiple_of(g * group_rows + x * tile, tile), tile)
-            if (j, dx) == (0, 0):
-                back_recv[i, landing, :] = back_send[i, there, :]
-            else:
-                remote(
-                    back_send.at[i, there, :],
-                    back_recv.at[i, landing, :],
-                    back_out_sem.at[0],
-                    back_in_sem.at[i],
-                    chip_at(j, dx) * 2 + core,
-                    z,
-                ).start()
+        if (j, h) == (0, 0):
+            there = pl.ds(pl.multiple_of(g * group_rows + lax.rem(chip_x, 2) * tile, tile), tile)
+            back_recv[i, landing, :] = back_send[i, there, :]
+        for to, x in chips_at(j, h):
+            there = pl.ds(pl.multiple_of(g * group_rows + lax.rem(x, 2) * tile, tile), tile)
+            remote(
+                back_send.at[i, there, :],
+                back_recv.at[i, landing, :],
+                back_out_sem.at[0],
+                back_in_sem.at[i],
+                to * 2 + core,
+                z,
+            ).start()
 
     for q in range(4):
         took(w_in_v.at[q], w_sem.at[q])
         took(w_out_v.at[q], w_sem.at[4 + q])
     order_of_work = (
-        (swap_planes, 0),
-        (swap_planes, 1),
-        (share, 0),
-        (swap_planes, 2),
-        (swap_planes, 3),
-        (share, 1),
+        (swap_planes, 0, 0),
+        (swap_planes, 0, 1),
+        (swap_planes, 1, 0),
+        (swap_planes, 1, 1),
+        (share, 0, 0),
+        (share, 0, 1),
+        (swap_planes, 2, 0),
+        (swap_planes, 2, 1),
+        (swap_planes, 3, 0),
+        (swap_planes, 3, 1),
+        (share, 1, 0),
+        (share, 1, 1),
         (compute, 0),
-        (share, 2),
-        (fold, 0),
-        (fold, 1),
-        (share, 3),
+        (share, 2, 0),
+        (share, 2, 1),
+        (fold, 0, 0),
+        (fold, 0, 1),
+        (fold, 1, 0),
+        (fold, 1, 1),
+        (share, 3, 0),
+        (share, 3, 1),
         (compute, 2),
-        (give_back, 0, 0),
-        (give_back, 0, 1),
-        (give_back, 1, 0),
-        (give_back, 1, 1),
-        (fold, 2),
-        (fold, 3),
-        (give_back, 2, 0),
-        (give_back, 3, 0),
-        (give_back, 2, 1),
-        (give_back, 3, 1),
+        (give_back, 0, 0, 0),
+        (give_back, 0, 0, 1),
+        (give_back, 0, 1, 0),
+        (give_back, 0, 1, 1),
+        (give_back, 1, 0, 0),
+        (give_back, 1, 0, 1),
+        (give_back, 1, 1, 0),
+        (give_back, 1, 1, 1),
+        (fold, 2, 0),
+        (fold, 2, 1),
+        (fold, 3, 0),
+        (fold, 3, 1),
+        (give_back, 2, 0, 0),
+        (give_back, 2, 1, 0),
+        (give_back, 3, 0, 0),
+        (give_back, 3, 1, 0),
+        (give_back, 2, 0, 1),
+        (give_back, 2, 1, 1),
+        (give_back, 3, 0, 1),
+        (give_back, 3, 1, 1),
     )
-    for work, *which in order_of_work:
-        work(steps[which[0]], *which[1:])
+    for work, k, *which in order_of_work:
+        work(steps[k], *which)
 
     for i in range(2):
         took(back_recv.at[i, pl.ds(0, half_rows - tile), :], back_in_sem.at[i])
@@ -363,6 +391,7 @@
     hidden = expert_in.shape[2]
     chips = sections // 2
     side = math.isqrt(chips)
+    groups = side * (side // 2)
     slice_width = width // inners
     q_width = width // 4
     rows_all = micro * rows
@@ -400,15 +429,15 @@
             dma((4,)),
             dma((8,)),
             dma((1,)),
-            dma((side,)),
-            dma((1,)),
-            dma((2, side)),
-            dma((1,)),
-            dma((2, side)),
-            dma((1,)),
-            dma((2, side)),
-            dma((1,)),
-            dma((2, side)),
+            dma((groups,)),
+            dma((1,)),
+            dma((2, groups)),
+            dma((1,)),
+            dma((2, groups)),
+            dma((1,)),
+            dma((2, groups)),
+            dma((1,)),
+            dma((2, groups)),
             dma((1,)),
             dma((2,)),
             dma((1,)),

time: 59.7 us -> 58.9 us (0.987)
  the two profiles are of different devices: /device:TPU:8 before, /device:TPU:6 now
where the time goes in v3:
time: 58.9 us; the launch traced here: 58.2 us
  Pallas kernels  56.9 us (97%)
  local copies, waits for them, and re-layouts  1.32 us (2%)
    pallas_call x1, Pallas kernels, body(): pl.pallas_call(functools.partial(moe_kernel, sections, inners, experts, m...  56.9 us
    unnamed x1, local copies, waits for them, and re-layouts  1.32 us

profile of v3, /device:TPU:6, one launch (start us, length us, event | category | flops | bytes accessed | tf_op | source)
XLA Modules:
  0.0 58.2 jit_solution(18124505652421780543)
XLA Ops:
  0.0 56.9 %shard_map.64 = bf16[32,192]{1,0:T(8,128)(2,1)} custom-call(bf16[32,3072]{1,0:T(8,128)(2,1)} %bitcast.9, f32[1,3072]{1,0:T(1,128)} %bitcast.12, bf16[8,3072]{1,0:T(8,128)(2,1)} %bitcast.11, s32[2,2,16]{2,1,0:T(2,128)} %bitcast.13, bf16[512,3072]{1,0:T(8,128)(2,1)} %bitcast.7, bf16[256,3072]{1,0:T(8,128)(2,1)} %bitcast.8), custom_call_target="tpu_custom_call" | custom-call | tf_op jit(solution)/shard_map/pallas_call | solution.py:403
  56.9 1.3 %copy.8 = bf16[2,16,192]{2,1,0:T(8,128)(2,1)} copy(bf16[2,16,192]{2,1,0:T(8,128)(2,1)} %bitcast.10) | data formatting | bytes 24576

commit v4 on v3

--- a/solution.py
+++ b/solution.py
@@ -66,6 +66,7 @@
     back_in_sem,
     part_out_sem,
     part_in_sem,
+    ready_sem,
 ):
     chips = sections // 2
     side = math.isqrt(chips)
@@ -136,8 +137,8 @@
             for to, _ in chips_at(j, h):
                 pl.semaphore_signal(barrier, inc=1, device_id=(to * 2 + core, z), device_id_type=MESH)
     pl.semaphore_signal(barrier, inc=1, device_id=(partner, z), device_id_type=MESH)
-    for k in range(1, inners):
-        pl.semaphore_signal(barrier, inc=1, device_id=(section, lax.rem(z + k, inners)), device_id_type=MESH)
+    for to in (z_up, z_down):
+        pl.semaphore_signal(barrier, inc=1, device_id=(section, to), device_id_type=MESH)
 
     for n, (src, dst) in enumerate(small):
         local(src, dst, small_sem.at[n]).wait()
@@ -178,7 +179,14 @@
     home = pl.ds(pl.multiple_of((my_group * 2 + core) * group_rows + lax.rem(chip_x, 2) * tile, tile), tile)
     slots[both, home, :] = outgoing[chip // per_expert]
 
-    pl.semaphore_wait(barrier, chips - 1 + 1 + inners - 1)
+    pl.semaphore_wait(barrier, chips - 1 + 1 + 2)
+
+    def tell_planes(n):
+        for to in (lax.rem(z + 2**n, inners), lax.rem(z + inners - 2**n, inners)):
+            pl.semaphore_signal(ready_sem.at[n], inc=1, device_id=(section, to), device_id_type=MESH)
+
+    rounds = (inners // 2).bit_length() - 1
+    tell_planes(0)
 
     for j in steps:
         for h in range(halves):
@@ -339,9 +347,15 @@
         (give_back, 3, 0, 1),
         (give_back, 3, 1, 1),
     )
-    for work, k, *which in order_of_work:
+    told = 0
+    for n, (work, k, *which) in enumerate(order_of_work):
         work(steps[k], *which)
-
+        if n in (3, 9) and told < rounds - 1:
+            pl.semaphore_wait(ready_sem.at[told], 2)
+            told += 1
+            tell_planes(told)
+
+    pl.semaphore_wait(ready_sem.at[rounds - 1], 2)
     for i in range(2):
         took(back_recv.at[i, pl.ds(0, half_rows - tile), :], back_in_sem.at[i])
         parts = jnp.dot(mix[...], back_recv[i], preferred_element_type=F32)
@@ -442,6 +456,7 @@
             dma((2,)),
             dma((1,)),
             dma((1,)),
+            pltpu.SemaphoreType.REGULAR(((inners // 2).bit_length() - 1,)),
         ],
         compiler_params=pltpu.CompilerParams(
             collective_id=0, has_side_effects=True, vmem_limit_bytes=62 * 1024 * 1024

time: 58.9 us -> 58.2 us (0.988)
  Pallas kernels: 56.9 us -> 56 us
    pallas_call x1, Pallas kernels: 56.9 us -> 56 us  [body(): pl.pallas_call(functools.partial(moe_kernel, sections, inners, experts, m...]
where the time goes in v4:
time: 58.2 us; the launch traced here: 57.4 us
  Pallas kernels  56 us (96%)
  local copies, waits for them, and re-layouts  1.32 us (2%)
    pallas_call x1, Pallas kernels, body(): pl.pallas_call(functools.partial(moe_kernel, sections, inners, experts, m...  56 us
    unnamed x1, local copies, waits for them, and re-layouts  1.32 us

profile of v4, /device:TPU:6, one launch (start us, length us, event | category | flops | bytes accessed | tf_op | source)
XLA Modules:
  0.0 57.4 jit_solution(187704397064791471)
XLA Ops:
  0.0 56.0 %shard_map.64 = bf16[32,192]{1,0:T(8,128)(2,1)} custom-call(bf16[32,3072]{1,0:T(8,128)(2,1)} %bitcast.9, f32[1,3072]{1,0:T(1,128)} %bitcast.12, bf16[8,3072]{1,0:T(8,128)(2,1)} %bitcast.11, s32[2,2,16]{2,1,0:T(2,128)} %bitcast.13, bf16[512,3072]{1,0:T(8,128)(2,1)} %bitcast.7, bf16[256,3072]{1,0:T(8,128)(2,1)} %bitcast.8), custom_call_target="tpu_custom_call" | custom-call | tf_op jit(solution)/shard_map/pallas_call | solution.py:417
  56.0 1.3 %copy.8 = bf16[2,16,192]{2,1,0:T(8,128)(2,1)} copy(bf16[2,16,192]{2,1,0:T(8,128)(2,1)} %bitcast.10) | data formatting | bytes 24576

commit v5 on v4

--- a/solution.py
+++ b/solution.py
@@ -132,13 +132,13 @@
     my_group = group_at(0, 0)
 
     barrier = pltpu.get_barrier_semaphore()
+    for to in (z_up, z_down):
+        pl.semaphore_signal(barrier, inc=1, device_id=(section, to), device_id_type=MESH)
     for j in steps:
         for h in range(halves):
             for to, _ in chips_at(j, h):
                 pl.semaphore_signal(barrier, inc=1, device_id=(to * 2 + core, z), device_id_type=MESH)
     pl.semaphore_signal(barrier, inc=1, device_id=(partner, z), device_id_type=MESH)
-    for to in (z_up, z_down):
-        pl.semaphore_signal(barrier, inc=1, device_id=(section, to), device_id_type=MESH)
 
     for n, (src, dst) in enumerate(small):
         local(src, dst, small_sem.at[n]).wait()
@@ -350,7 +350,7 @@
     told = 0
     for n, (work, k, *which) in enumerate(order_of_work):
         work(steps[k], *which)
-        if n in (3, 9) and told < rounds - 1:
+        if n in (1, 5) and told < rounds - 1:
             pl.semaphore_wait(ready_sem.at[told], 2)
             told += 1
             tell_planes(told)

time: 58.2 us -> 58.2 us (level)
  the two profiles are of different devices: /device:TPU:6 before, /device:TPU:2 now
where the time goes in v5:
time: 58.2 us; the launch traced here: 58.1 us
  Pallas kernels  56.7 us (97%)
  local copies, waits for them, and re-layouts  1.32 us (2%)
    pallas_call x1, Pallas kernels, body(): pl.pallas_call(functools.partial(moe_kernel, sections, inners, experts, m...  56.7 us
    unnamed x1, local copies, waits for them, and re-layouts  1.32 us

profile of v5, /device:TPU:2, one launch (start us, length us, event | category | flops | bytes accessed | tf_op | source)
XLA Modules:
  0.0 58.1 jit_solution(10201255689985125684)
XLA Ops:
  0.0 56.7 %shard_map.64 = bf16[32,192]{1,0:T(8,128)(2,1)} custom-call(bf16[32,3072]{1,0:T(8,128)(2,1)} %bitcast.9, f32[1,3072]{1,0:T(1,128)} %bitcast.12, bf16[8,3072]{1,0:T(8,128)(2,1)} %bitcast.11, s32[2,2,16]{2,1,0:T(2,128)} %bitcast.13, bf16[512,3072]{1,0:T(8,128)(2,1)} %bitcast.7, bf16[256,3072]{1,0:T(8,128)(2,1)} %bitcast.8), custom_call_target="tpu_custom_call" | custom-call | tf_op jit(solution)/shard_map/pallas_call | solution.py:417
  56.7 1.3 %copy.8 = bf16[2,16,192]{2,1,0:T(8,128)(2,1)} copy(bf16[2,16,192]{2,1,0:T(8,128)(2,1)} %bitcast.10) | data formatting | bytes 24576
